TPU v7x, 256 devices: a whole 4x4x8 slice. The times are simulated.
256 devices in a mesh: ctx: 64 (over x, z, y_lo), exp: 4 (over y_hi, core).
Axes of the slice: x: 4, y: 4 (y_hi: 2, y_lo: 2; y = y_hi * 2 + y_lo), z: 8, core: 2. Of those that a mesh axis runs over, the one named last changes fastest.
Arguments:
- query_rows: bfloat16 [32768, 3072], P(('ctx', 'exp')), may hold values from -6 to 6
- key_rows: bfloat16 [32768, 512], P('ctx'), may hold values from -6 to 6
- value_matrix: bfloat16 [32768, 512], P('ctx'), may hold values from -6 to 6
- out_grads: bfloat16 [32768, 3072], P(('ctx', 'exp')), may hold values from -6 to 6
- doc_start: int32 [32768], P(('ctx', 'exp')), may hold values from 0 to 32767, as said below
- moe_grads: bfloat16 [32768, 6144], P(('ctx', 'exp')), may hold values from -6 to 6
- expert_out: bfloat16 [32768, 2, 6144], P(('ctx', 'exp')), may hold values from -0.079589844 to 0.079589844
- gate_logits: float32 [32768, 2], P(('ctx', 'exp')), may hold values from -8 to 8
- routes: int32 [32768, 2], P(('ctx', 'exp')), may hold values from 0 to 7, all different within a row; in each aligned block of 128 rows (0 to 127, 128 to 255, ...) at most 40 rows name the same one
Outputs:
- query_grads: bfloat16 [32768, 3072], P(('ctx', 'exp'))
- key_grads: bfloat16 [32768, 512], P('ctx', 'exp')
- value_grads: bfloat16 [32768, 512], P('ctx', 'exp')
- expert_grads: bfloat16 [64, 8, 4, 40, 6144], P('ctx', 'exp')
- logit_grads: float32 [32768, 2], P(('ctx', 'exp'))
Inputs may be any that keep to these rules, and one draw needn't show every extreme that they name: doc_start[t] is the first position of the document that holds position t: at most t, never falling along the sequence, equal to t where a document begins; position 0 begins one, and so does the last position. `routes`: each token names two different experts; within each aligned block of 128 tokens (the tokens of one device) no expert is named by more than 40 tokens, a bound that some block reaches.
All inputs are finite; a program needn't handle non-finite values.
Results may differ from a plain program's by a relative error of at most 0.02.
Values may be sent and summed in bfloat16 or wider, within the bound.
No kernel may reach another device: no remote copies, remote signals or barrier semaphores. Data moves between devices by JAX's collectives and lax.ppermute only.
A program may use at most 192 MiB of HBM per device.

v0:
```python
import math

import jax
import jax.numpy as jnp
from jax import lax
from jax.sharding import PartitionSpec as P

HEAD_SIZE = 128
EXPERTS = 8
CAP = 40


def from_behind(block, axis, distance):
    devices = range(lax.axis_size(axis))
    route = [(i - distance, i) for i in devices if i - distance in devices]
    return lax.ppermute(block, axis, route)


def attend(query_block, grad_block, key_block, value_block, allowed):
    heads = query_block.shape[1] // HEAD_SIZE
    groups = key_block.shape[1] // HEAD_SIZE
    share = heads // groups
    count_rows = query_block.shape[0]
    count_keys = key_block.shape[0]
    factor = 1.0 / math.sqrt(HEAD_SIZE)
    queries = query_block.reshape(count_rows, groups, share, HEAD_SIZE)
    grads = grad_block.reshape(count_rows, groups, share, HEAD_SIZE)
    key_heads = key_block.reshape(count_keys, groups, HEAD_SIZE)
    value_heads = value_block.reshape(count_keys, groups, HEAD_SIZE)
    scores = (
        jnp.einsum("rgjd,sgd->gjrs", queries, key_heads, preferred_element_type=jnp.float32)
        * factor
    )
    scores = jnp.where(allowed[None, None], scores, -jnp.inf)
    peak = jnp.max(scores, axis=-1, keepdims=True)
    weights = jnp.exp(scores - peak)
    probs = weights / jnp.sum(weights, axis=-1, keepdims=True)
    probs_low = probs.astype(jnp.bfloat16)
    output = jnp.einsum(
        "gjrs,sgd->rgjd", probs_low, value_heads, preferred_element_type=jnp.float32
    )
    delta = jnp.einsum("rgjd,rgjd->gjr", grads.astype(jnp.float32), output)
    dprobs = jnp.einsum("rgjd,sgd->gjrs", grads, value_heads, preferred_element_type=jnp.float32)
    dscores_low = (probs * (dprobs - delta[..., None])).astype(jnp.bfloat16)
    query_grad = (
        jnp.einsum("gjrs,sgd->rgjd", dscores_low, key_heads, preferred_element_type=jnp.float32)
        * factor
    )
    key_grad = (
        jnp.einsum("gjrs,rgjd->sgd", dscores_low, queries, preferred_element_type=jnp.float32)
        * factor
    )
    value_grad = jnp.einsum("gjrs,rgjd->sgd", probs_low, grads, preferred_element_type=jnp.float32)
    query_grad = query_grad.reshape(count_rows, heads * HEAD_SIZE).astype(jnp.bfloat16)
    return (
        query_grad,
        key_grad.reshape(count_keys, groups * HEAD_SIZE),
        value_grad.reshape(count_keys, groups * HEAD_SIZE),
    )


def slot_numbers(flat_routes):
    onehot = (flat_routes[..., None] == jnp.arange(EXPERTS, dtype=jnp.int32)).astype(jnp.int32)
    before = jnp.cumsum(onehot, axis=-2) - onehot
    return jnp.sum(before * onehot, axis=-1)


def gated_rows(grad_rows, logits):
    gate = jax.nn.sigmoid(logits - logits[:, ::-1])
    scaled = (gate[:, :, None] * grad_rows[:, None, :]).astype(jnp.bfloat16)
    return (gate, scaled.reshape(grad_rows.shape[0] * 2, grad_rows.shape[1]))


def local(
    query_rows,
    key_rows,
    value_matrix,
    out_grads,
    doc_start,
    moe_grads,
    expert_out,
    gate_logits,
    routes,
):
    block_len = key_rows.shape[0]
    count_rows = query_rows.shape[0]
    width = moe_grads.shape[1]
    ctx_pos = lax.axis_index("ctx")
    exp_pos = lax.axis_index("exp")
    group_count = lax.axis_size("exp")
    prev_keys, prev_values = from_behind((key_rows, value_matrix), "ctx", 1)
    both_keys = jnp.concatenate([prev_keys, key_rows], axis=0)
    both_values = jnp.concatenate([prev_values, value_matrix], axis=0)
    query_pos = ctx_pos * block_len + exp_pos * count_rows + jnp.arange(count_rows, dtype=jnp.int32)
    key_pos = (ctx_pos - 1) * block_len + jnp.arange(2 * block_len, dtype=jnp.int32)
    allowed = (key_pos[None, :] >= doc_start[:, None]) & (key_pos[None, :] <= query_pos[:, None])
    query_grads, key_part, value_part = attend(
        query_rows, out_grads, both_keys, both_values, allowed
    )
    key_prev, key_own = (key_part[:block_len], key_part[block_len:])
    value_prev, value_own = (value_part[:block_len], value_part[block_len:])
    back_key, back_value = from_behind((key_prev, value_prev), "ctx", -1)
    key_total, value_total = (
        lax.psum_scatter(key_own + back_key, "exp", scatter_dimension=1, tiled=True),
        lax.psum_scatter(value_own + back_value, "exp", scatter_dimension=1, tiled=True),
    )
    key_grads = key_total.astype(jnp.bfloat16)
    value_grads = value_total.astype(jnp.bfloat16)
    gate, scaled = gated_rows(moe_grads, gate_logits)
    local_experts = EXPERTS // group_count
    flat_routes = routes.reshape(1, 2 * count_rows)
    slots = slot_numbers(flat_routes)
    token_position = (flat_routes * CAP + slots).reshape(-1)
    send = jnp.zeros((EXPERTS * CAP, width), jnp.bfloat16).at[token_position].set(scaled)
    received = lax.all_to_all(
        send.reshape(EXPERTS, 1, CAP, width), "exp", split_axis=0, concat_axis=1, tiled=True
    )
    expert_grads = received.reshape(1, local_experts, group_count, CAP, width)
    gate_grad = jnp.einsum("td,tad->ta", moe_grads, expert_out, preferred_element_type=jnp.float32)
    logit_grads = gate * (gate_grad - jnp.sum(gate * gate_grad, axis=-1, keepdims=True))
    return (query_grads, key_grads, value_grads, expert_grads, logit_grads)


def solution(mesh):
    in_specs = (
        P(("ctx", "exp"), None),
        P("ctx", None),
        P("ctx", None),
        P(("ctx", "exp"), None),
        P(("ctx", "exp")),
        P(("ctx", "exp"), None),
        P(("ctx", "exp"), None, None),
        P(("ctx", "exp"), None),
        P(("ctx", "exp"), None),
    )
    out_specs = (
        P(("ctx", "exp"), None),
        P("ctx", "exp"),
        P("ctx", "exp"),
        P("ctx", "exp", None, None, None),
        P(("ctx", "exp"), None),
    )
    return jax.shard_map(local, mesh=mesh, in_specs=in_specs, out_specs=out_specs, check_vma=False)
```

profile of v0, /device:TPU:103, one launch (start us, length us, event | category | flops | bytes accessed | tf_op | source)
XLA Modules:
  0.0 217.3 jit_solution(5191174831381660972)
XLA Ops:
  7.2 2.2 %copy.49 = bf16[512,512]{0,1:T(8,128)(2,1)} copy(bf16[512,512]{1,0:T(8,128)(2,1)} %param.10) | data formatting | bytes 1048576 | tf_op args[1]
  9.4 3.2 %collective-permute-start = (bf16[512,512]{0,1:T(8,128)(2,1)}, bf16[512,512]{0,1:T(8,128)(2,1)}, u32[]{:S(2)}, u32[]{:S(2)}) collective-permute-start(bf16[512,512]{0,1:T(8,128)(2,1)} %copy.49), channel_id=1, source_target_pairs={{0,4},{4,8},{8,12},{12,16},{16,20},{20,24},{24,28},{28,32},{32,36}... | collective-permute-start | bytes 1572872 | tf_op jit(solution)/shard_map/ppermute | solution.py:16
  12.6 2.0 copy.54
  14.7 4.6 %collective-permute-start.1 = (bf16[512,512]{0,1:T(8,128)(2,1)}, bf16[512,512]{0,1:T(8,128)(2,1)}, u32[]{:S(2)}, u32[]{:S(2)}) collective-permute-start(bf16[512,512]{0,1:T(8,128)(2,1)} %copy.54), channel_id=1, source_target_pairs={{0,4},{4,8},{8,12},{12,16},{16,20},{20,24},{24,28},{28,32},{32,36}... | collective-permute-start | bytes 1572872 | tf_op jit(solution)/shard_map/ppermute | solution.py:16
  19.3 2.3 %copy.51 = bf16[128,3072]{0,1:T(8,128)(2,1)} copy(bf16[128,3072]{1,0:T(8,128)(2,1)} %param.9) | data formatting | bytes 1572864 | tf_op args[0]
  21.6 2.3 %copy.56 = bf16[128,3072]{0,1:T(8,128)(2,1)} copy(bf16[128,3072]{1,0:T(8,128)(2,1)} %param.12) | data formatting | bytes 1572864 | tf_op args[3]
  25.3 2.4 %pad_maximum_fusion = bf16[1024,512]{0,1:T(8,128)(2,1)} fusion(bf16[512,512]{0,1:T(8,128)(2,1)} %copy.49, bf16[512,512]{0,1:T(8,128)(2,1)} %collective-permute-done), kind=kLoop, calls=%fused_computation.26 | loop fusion | flops 2097152 | bytes 2097152 | tf_op jit(solution)/shard_map/concatenate | solution.py:92
  27.7 9.8 %fusion.25 = (f32[4,6,128]{2,1,0:T(8,128)S(1)}, f32[4,6,128,1024]{2,3,1,0:T(8,128)}) fusion(pred[128,1024]{0,1:T(8,128)(4,1)S(1)} %compare_and_fusion, bf16[1024,4,128,1]{0,2,3,1:T(8,128)(2,1)} %bitcast.117, bf16[128,4,6,128]{0,3,2,1:T(8,128)(2,1)} %bitcast.121), kind=kOutput, calls=%fused_computation.50 | convolution fusion | flops 817890304 | bytes 14561280 | tf_op jit(solution)/shard_map/sub | solution.py:36
  37.6 8.8 %fusion.7 = bf16[4,6,128,1024]{2,3,1,0:T(8,128)(2,1)} fusion(f32[4,6,128,1024]{2,3,1,0:T(8,128)} %get-tuple-element.27, f32[4,6,128]{2,1,0:T(8,128)S(1)} %get-tuple-element.26), kind=kLoop, calls=%fused_computation.13 | loop fusion | flops 6291456 | bytes 18886656 | tf_op jit(solution)/shard_map/convert_element_type | solution.py:38
  47.6 3.9 %fusion.14 = f32[4,6,128]{2,1,0:T(8,128)S(1)} fusion(bf16[4,6,128,128]{2,3,1,0:T(8,128)(2,1)S(1)} %bitcast.110, bf16[1024,4,128,1]{0,2,3,1:T(8,128)(2,1)S(1)} %bitcast.119, bf16[4,6,128,1024]{2,3,1,0:T(8,128)(2,1)} %fusion.7), kind=kOutput, calls=%fused_computation.23 | convolution fusion | flops 806482944 | bytes 8138752 | tf_op jit(solution)/shard_map/gjrs,sgd->rgjd/dot_general | solution.py:39
  51.5 5.9 %fusion.2 = bf16[4,6,128,1024]{2,3,1,0:T(8,128)(2,1)S(1)} fusion(f32[4,6,128]{2,1,0:T(8,128)S(1)} %fusion.14, f32[4,6,128,1024]{2,3,1,0:T(8,128)} %get-tuple-element.27, f32[4,6,128]{2,1,0:T(8,128)S(1)} %get-tuple-element.26, bf16[1024,4,128,1]{0,2,3,1:T(8,128)(2,1)S(1)} %bitcast.120, bf16[128,4,6,128]{0,3,2,1:T(8,128)(2,1)S(1)} %bitcast.111), kind=kOutput, calls=%fused_computation.4 | convolution fusion | flops 817889280 | bytes 20733952 | tf_op jit(solution)/shard_map/rgjd,sgd->gjrs/dot_general | solution.py:43
  57.4 2.2 fusion.12
  61.6 2.6 %copy.62 = f32[512,512]{1,0:T(8,128)} copy(f32[512,512]{0,1:T(8,128)} %bitcast.115) | data formatting | bytes 2097152 | tf_op jit(solution)/shard_map/slice | solution.py:100
  64.2 2.1 collective-permute-start.2
  66.3 8.6 %fusion.10 = f32[128,1,2]{2,1,0:T(1,128)S(1)} fusion(bf16[128,2,6144]{2,1,0:T(2,128)(2,1)S(1)} %copy-done, bf16[128,6144,1]{1,0,2:T(8,128)(2,1)} %bitcast.124), kind=kOutput, calls=%fused_computation.16 | convolution fusion | flops 3145728 | bytes 4719616 | tf_op jit(solution)/shard_map/td,tad->ta/dot_general | solution.py:119
  76.2 1.6 copy.63
  77.8 10.7 %collective-permute-done.2 = f32[512,512]{1,0:T(8,128)} collective-permute-done((f32[512,512]{1,0:T(8,128)}, f32[512,512]{1,0:T(8,128)}, u32[]{:S(2)}, u32[]{:S(2)}) %collective-permute-start.2) | collective-permute-done | bytes 1048608 | tf_op jit(solution)/shard_map/ppermute | solution.py:16
  88.5 2.4 %add.68 = f32[512,512]{1,0:T(8,128)} add(f32[512,512]{1,0:T(8,128)S(1)} %copy.63, f32[512,512]{1,0:T(8,128)} %collective-permute-done.2) | non-fusion elementwise | flops 262144 | bytes 3145728 | tf_op jit(solution)/shard_map/add | solution.py:104
  91.4 5.2 %mul.101 = f32[128,2,6144]{2,1,0:T(2,128)} broadcast(bf16[128,6144]{1,0:T(8,128)(2,1)S(1)} %copy-done.8), dimensions={0,2} | broadcast | bytes 7864320 | tf_op jit(solution)/shard_map/mul | solution.py:70
  96.7 8.4 %mul.102 = f32[256,6144]{1,0:T(8,128)} reshape(f32[128,2,6144]{2,1,0:T(2,128)} %mul.101) | data formatting | bytes 12582912 | tf_op jit(solution)/shard_map/mul | solution.py:70
  105.1 4.9 %convolution_bitcast_fusion = f32[1024,4,128]{0,2,1:T(8,128)S(1)} fusion(bf16[4,6,128,1024]{2,3,1,0:T(8,128)(2,1)} %fusion.7, bf16[128,4,6,128]{0,3,2,1:T(8,128)(2,1)S(1)} %bitcast.112), kind=kOutput, calls=%fused_computation.21 | convolution fusion | flops 805306368 | bytes 9175040 | tf_op jit(solution)/shard_map/gjrs,rgjd->sgd/dot_general | solution.py:53
  111.3 2.5 %copy.65 = f32[512,512]{1,0:T(8,128)} copy(f32[512,512]{0,1:T(8,128)} %bitcast.116) | data formatting | bytes 2097152 | tf_op jit(solution)/shard_map/slice | solution.py:101
  113.8 3.1 %collective-permute-start.3 = (f32[512,512]{1,0:T(8,128)}, f32[512,512]{1,0:T(8,128)}, u32[]{:S(2)}, u32[]{:S(2)}) collective-permute-start(f32[512,512]{1,0:T(8,128)} %copy.65), channel_id=1, source_target_pairs={{4,0},{8,4},{12,8},{16,12},{20,16},{24,20},{28,24},{32,28},{36,32}... | collective-permute-start | bytes 3145736 | tf_op jit(solution)/shard_map/ppermute | solution.py:16
  117.0 9.4 %scatter_custom_fusion = bf16[320,6144]{1,0:T(8,128)(2,1)} fusion(s32[256]{0:T(256)S(1)} %bitcast.127, f32[256,6144]{1,0:T(8,128)} %mul.102, f32[256]{0:T(256)S(1)} %mul.99, bf16[]{:T(256)} %constant.12.clone.1), kind=kCustom, calls=%fused_computation.14 | custom fusion | flops 3145728 | bytes 10224642 | tf_op jit(solution)/shard_map/scatter | solution.py:114
  126.4 8.8 %all-to-all-start = ((bf16[8,1,40,6144]{3,2,1,0:T(8,128)(2,1)}), bf16[8,1,40,6144]{3,2,1,0:T(8,128)(2,1)}, u32[]{:S(2)}, u32[]{:S(2)}) async-start(bf16[8,1,40,6144]{3,2,1,0:T(8,128)(2,1)} %bitcast.109), calls=%async_computation.2 | async-start | bytes 7864320 | tf_op jit(solution)/shard_map/all_to_all | solution.py:115
  135.5 11.0 %collective-permute-done.3 = f32[512,512]{1,0:T(8,128)} collective-permute-done((f32[512,512]{1,0:T(8,128)}, f32[512,512]{1,0:T(8,128)}, u32[]{:S(2)}, u32[]{:S(2)}) %collective-permute-start.3) | collective-permute-done | bytes 1048608 | tf_op jit(solution)/shard_map/ppermute | solution.py:16
  146.5 2.4 %add.69 = f32[512,512]{1,0:T(8,128)} add(f32[512,512]{1,0:T(8,128)S(1)} %copy.66, f32[512,512]{1,0:T(8,128)} %collective-permute-done.3) | non-fusion elementwise | flops 262144 | bytes 3145728 | tf_op jit(solution)/shard_map/add | solution.py:105
  149.5 3.8 %multiply_convert_fusion.2 = bf16[4,128,6,128]{3,1,2,0:T(8,128)(2,1)S(1)} fusion(bf16[1024,4,128,1]{0,2,3,1:T(8,128)(2,1)S(1)} %bitcast.118, bf16[4,6,128,1024]{2,3,1,0:T(8,128)(2,1)} %copy-done.2), kind=kOutput, calls=%fused_computation.24 | convolution fusion | flops 806092800 | bytes 8126464 | tf_op jit(solution)/shard_map/gjrs,sgd->rgjd/dot_general | solution.py:46
  154.5 48.0 %all-to-all-done = bf16[8,1,40,6144]{3,2,1,0:T(8,128)(2,1)} async-done(((bf16[8,1,40,6144]{3,2,1,0:T(8,128)(2,1)}), bf16[8,1,40,6144]{3,2,1,0:T(8,128)(2,1)}, u32[]{:S(2)}, u32[]{:S(2)}) %all-to-all-start) | async-done | bytes 3932192 | tf_op jit(solution)/shard_map/all_to_all | solution.py:115
  202.5 4.6 %copy.71 = bf16[1,2,4,40,6144]{4,3,2,1,0:T(8,128)(2,1)} copy(bf16[1,2,4,40,6144]{4,3,1,2,0:T(8,128)(2,1)} %bitcast.42) | data formatting | bytes 7864320
  207.2 1.6 convert_element_type.46
  208.8 1.6 convert_element_type.47
  (58 shorter events, 9.9 us)
Async XLA Ops:
  7.2 59.2 %copy-start = (bf16[128,2,6144]{2,1,0:T(2,128)(2,1)S(1)}, bf16[128,2,6144]{2,1,0:T(2,128)(2,1)}, u32[]{:S(2)}) copy-start(bf16[128,2,6144]{2,1,0:T(2,128)(2,1)} %param.15) | copy-start | bytes 9437188
  7.2 16.7 %copy-start.11 = (s32[128]{0:T(128)S(1)}, s32[128]{0:T(128)}, u32[]{:S(2)}) copy-start(s32[128]{0:T(128)} %param.13) | copy-start | bytes 1540
  7.2 200.0 %reduce-scatter.3.cloned.1.call-start = ((), (), s32[]{:S(2)}) async-start(), calls=%async_computation.3 | async-start | bytes 1310720 | tf_op jit(solution)/shard_map/reduce_scatter | solution.py:104
  9.4 15.9 %collective-permute-start = (bf16[512,512]{0,1:T(8,128)(2,1)}, bf16[512,512]{0,1:T(8,128)(2,1)}, u32[]{:S(2)}, u32[]{:S(2)}) collective-permute-start(bf16[512,512]{0,1:T(8,128)(2,1)} %copy.49), channel_id=1, source_target_pairs={{0,4},{4,8},{8,12},{12,16},{16,20},{20,24},{24,28},{28,32},{32,36}... | collective-permute-start | bytes 1572872 | tf_op jit(solution)/shard_map/ppermute | solution.py:16
  14.7 31.7 %collective-permute-start.1 = (bf16[512,512]{0,1:T(8,128)(2,1)}, bf16[512,512]{0,1:T(8,128)(2,1)}, u32[]{:S(2)}, u32[]{:S(2)}) collective-permute-start(bf16[512,512]{0,1:T(8,128)(2,1)} %copy.54), channel_id=1, source_target_pairs={{0,4},{4,8},{8,12},{12,16},{16,20},{20,24},{24,28},{28,32},{32,36}... | collective-permute-start | bytes 1572872 | tf_op jit(solution)/shard_map/ppermute | solution.py:16
  37.6 8.9 %copy-start.7 = (bf16[512,512]{0,1:T(8,128)(2,1)S(1)}, bf16[512,512]{0,1:T(8,128)(2,1)}, u32[]{:S(2)}) copy-start(bf16[512,512]{0,1:T(8,128)(2,1)} %copy.54) | copy-start | bytes 1572868
  37.6 10.0 %copy-start.3 = (bf16[128,3072]{0,1:T(8,128)(2,1)S(1)}, bf16[128,3072]{0,1:T(8,128)(2,1)}, u32[]{:S(2)}) copy-start(bf16[128,3072]{0,1:T(8,128)(2,1)} %copy.56) | copy-start | bytes 2359300
  51.5 5.9 %copy-start.6 = (bf16[128,3072]{0,1:T(8,128)(2,1)S(1)}, bf16[128,3072]{0,1:T(8,128)(2,1)}, u32[]{:S(2)}) copy-start(bf16[128,3072]{0,1:T(8,128)(2,1)} %copy.51) | copy-start | bytes 2359300
  57.4 2.7 %copy-start.2 = (bf16[4,6,128,1024]{2,3,1,0:T(8,128)(2,1)}, bf16[4,6,128,1024]{2,3,1,0:T(8,128)(2,1)S(1)}, u32[]{:S(2)}) copy-start(bf16[4,6,128,1024]{2,3,1,0:T(8,128)(2,1)S(1)} %fusion.2) | copy-start | bytes 18874372
  64.2 24.3 %collective-permute-start.2 = (f32[512,512]{1,0:T(8,128)}, f32[512,512]{1,0:T(8,128)}, u32[]{:S(2)}, u32[]{:S(2)}) collective-permute-start(f32[512,512]{1,0:T(8,128)} %copy.62), channel_id=1, source_target_pairs={{4,0},{8,4},{12,8},{16,12},{20,16},{24,20},{28,24},{32,28},{36,32}... | collective-permute-start | bytes 3145736 | tf_op jit(solution)/shard_map/ppermute | solution.py:16
  66.3 8.6 %copy-start.9 = (s32[128,2]{0,1:T(2,128)S(1)}, s32[128,2]{0,1:T(2,128)}, u32[]{:S(2)}) copy-start(s32[128,2]{0,1:T(2,128)} %param.17) | copy-start | bytes 3076
  66.3 9.8 %copy-start.10 = (f32[128,2]{0,1:T(2,128)S(1)}, f32[128,2]{0,1:T(2,128)}, u32[]{:S(2)}) copy-start(f32[128,2]{0,1:T(2,128)} %param.16) | copy-start | bytes 3076
  75.0 16.5 %copy-start.8 = (bf16[128,6144]{1,0:T(8,128)(2,1)S(1)}, bf16[128,6144]{1,0:T(8,128)(2,1)}, u32[]{:S(2)}) copy-start(bf16[128,6144]{1,0:T(8,128)(2,1)} %param.14) | copy-start | bytes 4718596
  96.7 8.5 %copy-start.4 = (bf16[128,3072]{0,1:T(8,128)(2,1)S(1)}, bf16[128,3072]{0,1:T(8,128)(2,1)}, u32[]{:S(2)}) copy-start(bf16[128,3072]{0,1:T(8,128)(2,1)} %copy.56) | copy-start | bytes 2359300
  113.8 32.7 %collective-permute-start.3 = (f32[512,512]{1,0:T(8,128)}, f32[512,512]{1,0:T(8,128)}, u32[]{:S(2)}, u32[]{:S(2)}) collective-permute-start(f32[512,512]{1,0:T(8,128)} %copy.65), channel_id=1, source_target_pairs={{4,0},{8,4},{12,8},{16,12},{20,16},{24,20},{28,24},{32,28},{36,32}... | collective-permute-start | bytes 3145736 | tf_op jit(solution)/shard_map/ppermute | solution.py:16
  126.4 76.1 %all-to-all-start = ((bf16[8,1,40,6144]{3,2,1,0:T(8,128)(2,1)}), bf16[8,1,40,6144]{3,2,1,0:T(8,128)(2,1)}, u32[]{:S(2)}, u32[]{:S(2)}) async-start(bf16[8,1,40,6144]{3,2,1,0:T(8,128)(2,1)} %bitcast.109), calls=%async_computation.2 | async-start | bytes 7864320 | tf_op jit(solution)/shard_map/all_to_all | solution.py:115
  135.2 14.3 %copy-start.5 = (bf16[1024,512]{0,1:T(8,128)(2,1)S(1)}, bf16[1024,512]{0,1:T(8,128)(2,1)}, u32[]{:S(2)}) copy-start(bf16[1024,512]{0,1:T(8,128)(2,1)} %pad_maximum_fusion) | copy-start | bytes 3145732
  135.2 73.6 %reduce-scatter.5.cloned.1.call-start = ((), (), s32[]{:S(2)}) async-start(), calls=%async_computation.4 | async-start | bytes 1310720 | tf_op jit(solution)/shard_map/reduce_scatter | solution.py:105
  202.5 7.9 %copy-start.1 = (bf16[128,2,6144]{2,1,0:T(2,128)(2,1)S(1)}, bf16[128,2,6144]{2,1,0:T(2,128)(2,1)}, u32[]{:S(2)}) copy-start(bf16[128,2,6144]{2,1,0:T(2,128)(2,1)} %param.15) | copy-start | bytes 9437188
Sparse Core Ops, SparseCore 0:
  91.0 69.9 reduce-scatter.2
  163.8 39.3 reduce-scatter.4
where the time goes:
time: 218 us; the launch traced here: 217 us
  waiting for transfers between devices  70.9 us (33%)
  local copies, waits for them, and re-layouts  39.6 us (18%)
  matrix products  39.1 us (18%)
  other arithmetic  31.4 us (14%)
  starting transfers between devices  21.9 us (10%)
  between operations  14.3 us (7%)
    all_to_all x1, waiting for transfers between devices, local(): lax.all_to_all(send.reshape(EXPERTS, 1, CAP, width), 'exp', split_axis=0,...  48 us
    ppermute x4, waiting for transfers between devices, from_behind(): return lax.ppermute(block, axis, route)  22.9 us
    unnamed x31, local copies, waits for them, and re-layouts  15.3 us
    mul x3, local copies, waits for them, and re-layouts, gated_rows(): scaled = (gate[:, :, None] * grad_rows[:, None, :]).astype(jnp.bfloat16)  13.7 us
    ppermute x4, starting transfers between devices, from_behind(): return lax.ppermute(block, axis, route)  13 us
    sub x1, matrix products, attend(): weights = jnp.exp(scores - peak)  9.84 us
    scatter x1, other arithmetic, local(): jnp.zeros((EXPERTS * CAP, width), jnp.bfloat16).at[token_position]  9.45 us
    convert_element_type x1, other arithmetic, attend(): probs_low = probs.astype(jnp.bfloat16)  8.85 us
  transfers between devices with their start and end apart: 7, of which 4 were waited for; matrix products, arithmetic and copies ran while one was open for 40% of the time, Pallas kernels for 0%

commit v1 on v0

v1 whole, which is shorter than its diff:
```python
import functools
import math

import jax
import jax.numpy as jnp
from jax import lax
from jax.experimental import pallas as pl
from jax.experimental.pallas import tpu as pltpu
from jax.sharding import PartitionSpec as P

HEAD_SIZE = 128
EXPERTS = 8
CAP = 40
AXES = ("ctx", "exp")
BLOCK = 512
SHARE = 6
CHUNK = 256
FACTOR = 1.0 / math.sqrt(HEAD_SIZE)
LOG2E = math.log2(math.e)
NEG = -1e30


def routes_of(fn):
    blocks, group = lax.axis_size("ctx"), lax.axis_size("exp")
    pairs = []
    for b in range(blocks):
        for e in range(group):
            tb, te = fn(b, e)
            pairs.append((b * group + e, (tb % blocks) * group + te))
    return pairs


def send(x, fn):
    return lax.ppermute(x, AXES, routes_of(fn))


def to_core(b, e):
    return b, e ^ 1


def to_cross(b, e):
    return b, e ^ 2


def to_next_same(b, e):
    return b + 1, e


def to_next_other(b, e):
    return b + 1, e ^ 2


def to_prev_same(b, e):
    return b - 1, e


def to_prev_other(b, e):
    return b - 1, e ^ 2


def pack_kv_kernel(s_ref, k_ref, v_ref, ko_ref, vo_ref):
    ko_ref[...] = k_ref[...]
    vo_ref[...] = v_ref[...]


def pack_kv(scal, keys, values):
    rows = keys.shape[0]
    pick = lambda g, s: (0, 2 * g + s[0])
    spec = pl.BlockSpec((rows, HEAD_SIZE), pick)
    out = pl.BlockSpec((rows, HEAD_SIZE), lambda g, s: (0, g))
    shape = jax.ShapeDtypeStruct((rows, 2 * HEAD_SIZE), keys.dtype)
    return pl.pallas_call(
        pack_kv_kernel,
        grid_spec=pltpu.PrefetchScalarGridSpec(
            num_scalar_prefetch=1, grid=(2,), in_specs=[spec, spec], out_specs=[out, out]
        ),
        out_shape=[shape, shape],
        name="pack_kv",
    )(scal, keys, values)


def pack_qg_kernel(s_ref, q_ref, g_ref, logit_ref, route_ref, doc_ref, out_ref, meta_ref):
    wide = q_ref.shape[1]
    out_ref[0, :, :wide] = q_ref[...]
    out_ref[0, :, wide:] = g_ref[...]

    @pl.when(pl.program_id(0) == 0)
    def _():
        tokens = logit_ref.shape[1]
        logits = logit_ref[...]
        routes = route_ref[...]
        l0, l1 = logits[0:1], logits[1:2]
        r0, r1 = routes[0:1], routes[1:2]
        gate0 = jax.nn.sigmoid(l0 - l1)
        gate1 = jax.nn.sigmoid(l1 - l0)
        expert = lax.broadcasted_iota(jnp.int32, (EXPERTS, tokens), 0)
        hit0 = (jnp.broadcast_to(r0, (EXPERTS, tokens)) == expert).astype(jnp.float32)
        hit1 = (jnp.broadcast_to(r1, (EXPERTS, tokens)) == expert).astype(jnp.float32)
        hits = hit0 + hit1
        earlier = (
            lax.broadcasted_iota(jnp.int32, (tokens, tokens), 0)
            < lax.broadcasted_iota(jnp.int32, (tokens, tokens), 1)
        ).astype(jnp.float32)
        before = jnp.dot(hits, earlier, preferred_element_type=jnp.float32)
        slot0 = jnp.sum(before * hit0, axis=0, keepdims=True)
        slot1 = jnp.sum(before * hit1, axis=0, keepdims=True)
        meta_ref[0:1] = r0.astype(jnp.float32) * CAP + slot0
        meta_ref[1:2] = r1.astype(jnp.float32) * CAP + slot1
        meta_ref[2:3] = gate0
        meta_ref[3:4] = gate1
        meta_ref[4:5] = doc_ref[...].astype(jnp.float32)
        meta_ref[5:8] = jnp.zeros((3, tokens), jnp.float32)


def pack_qg(scal, queries, grads, logits_t, routes_t, doc_row):
    rows, width = queries.shape
    wide = SHARE * HEAD_SIZE
    pick = lambda g, s: (0, 2 * g + 1 - s[0])
    whole = lambda a: pl.BlockSpec(a.shape, lambda g, s: (0, 0))
    return pl.pallas_call(
        pack_qg_kernel,
        grid_spec=pltpu.PrefetchScalarGridSpec(
            num_scalar_prefetch=1,
            grid=(2,),
            in_specs=[
                pl.BlockSpec((rows, wide), pick),
                pl.BlockSpec((rows, wide), pick),
                whole(logits_t),
                whole(routes_t),
                whole(doc_row),
            ],
            out_specs=[
                pl.BlockSpec((1, rows, 2 * wide), lambda g, s: (g, 0, 0)),
                pl.BlockSpec((8, rows), lambda g, s: (0, 0)),
            ],
        ),
        out_shape=[
            jax.ShapeDtypeStruct((2, rows, 2 * wide), queries.dtype),
            jax.ShapeDtypeStruct((8, rows), jnp.float32),
        ],
        name="pack_qg",
    )(scal, queries, grads, logits_t, routes_t, doc_row)


def nt(a, b):
    return lax.dot_general(a, b, (((1,), (1,)), ((), ())), preferred_element_type=jnp.float32)


def attend_kernel(
    heads_per_step,
    s_ref,
    q_ref,
    g_ref,
    qp_ref,
    gp_ref,
    kp_ref,
    ko_ref,
    vp_ref,
    vo_ref,
    meta_ref,
    metap_ref,
    dqo_ref,
    dqp_ref,
    prev_ref,
    own_ref,
    bias,
    kt,
    score,
    grad,
    low,
    dk,
    dv,
):
    step = pl.program_id(0)
    rows = q_ref.shape[0]
    tokens = 2 * rows
    span = kp_ref.shape[0]
    half = span // CHUNK

    def keys(c):
        return kp_ref[pl.ds(c * CHUNK, CHUNK), :] if c < half else ko_ref[pl.ds((c - half) * CHUNK, CHUNK), :]

    def values(c):
        return vp_ref[pl.ds(c * CHUNK, CHUNK), :] if c < half else vo_ref[pl.ds((c - half) * CHUNK, CHUNK), :]

    @pl.when(step == 0)
    def _():
        core, side, ctx = s_ref[0], s_ref[1], s_ref[2]
        base = (ctx - 1) * span
        mine = ctx * span + (2 * side + core) * rows
        theirs = ctx * span + (2 * side + 1 - core) * rows
        lane = lax.broadcasted_iota(jnp.int32, (1, rows), 1)
        qpos = jnp.concatenate([mine + lane, theirs + lane], axis=1)
        doc = jnp.concatenate([meta_ref[4:5], metap_ref[4:5]], axis=1).astype(jnp.int32)
        for c in range(2 * half):
            kpos = base + c * CHUNK + lax.broadcasted_iota(jnp.int32, (CHUNK, tokens), 0)
            ok = (kpos >= doc) & (kpos <= qpos)
            bias[pl.ds(c * CHUNK, CHUNK), :] = jnp.where(ok, 0.0, NEG)
            kt[:, pl.ds(c * CHUNK, CHUNK)] = keys(c).T
        dk[...] = jnp.zeros_like(dk)
        dv[...] = jnp.zeros_like(dv)

    for h in range(heads_per_step):
        cols = slice(h * HEAD_SIZE, (h + 1) * HEAD_SIZE)
        q2 = jnp.concatenate([q_ref[:, cols], qp_ref[0, :, cols]], axis=0)
        g2 = jnp.concatenate([g_ref[:, cols], gp_ref[0, :, cols]], axis=0)
        peak = None
        for c in range(2 * half):
            at = pl.ds(c * CHUNK, CHUNK)
            s = nt(keys(c), q2) * (FACTOR * LOG2E) + bias[at, :]
            score[h, at, :] = s
            top = jnp.max(s, axis=0, keepdims=True)
            peak = top if peak is None else jnp.maximum(peak, top)
        total = None
        for c in range(2 * half):
            at = pl.ds(c * CHUNK, CHUNK)
            w = jnp.exp2(score[h, at, :] - peak)
            score[h, at, :] = w
            part = jnp.sum(w, axis=0, keepdims=True)
            total = part if total is None else total + part
        inv = 1.0 / total
        delta = None
        for c in range(2 * half):
            at = pl.ds(c * CHUNK, CHUNK)
            p = score[h, at, :] * inv
            score[h, at, :] = p
            pl_low = p.astype(jnp.bfloat16)
            low[h, at, :] = pl_low
            dp = nt(values(c), g2)
            grad[h, at, :] = dp
            part = jnp.sum(pl_low.astype(jnp.float32) * dp, axis=0, keepdims=True)
            delta = part if delta is None else delta + part
        dqt = None
        for c in range(2 * half):
            at = pl.ds(c * CHUNK, CHUNK)
            ds = (score[h, at, :] * (grad[h, at, :] - delta)).astype(jnp.bfloat16)
            dk[at, :] += jnp.dot(ds, q2, preferred_element_type=jnp.float32)
            dv[at, :] += jnp.dot(low[h, at, :], g2, preferred_element_type=jnp.float32)
            part = jnp.dot(kt[:, at], ds, preferred_element_type=jnp.float32)
            dqt = part if dqt is None else dqt + part
        dq = (dqt * FACTOR).T.astype(jnp.bfloat16)
        dqo_ref[:, cols] = dq[:rows]
        dqp_ref[:, cols] = dq[rows:]

    @pl.when(step == pl.num_programs(0) - 1)
    def _():
        prev_ref[:, :HEAD_SIZE] = (dk[:span, :] * FACTOR).astype(prev_ref.dtype)
        prev_ref[:, HEAD_SIZE:] = dv[:span, :].astype(prev_ref.dtype)
        own_ref[:, :HEAD_SIZE] = (dk[span:, :] * FACTOR).astype(own_ref.dtype)
        own_ref[:, HEAD_SIZE:] = dv[span:, :].astype(own_ref.dtype)


def attend(scal, queries, grads, payload, keys_prev, keys, values_prev, values, meta, meta_core, which, own_dtype, name):
    heads_per_step = 2
    steps = SHARE // heads_per_step
    rows = queries.shape[0]
    span = keys.shape[0]
    wide = heads_per_step * HEAD_SIZE
    qcol = lambda j, s: (0, steps * (2 * s[3] + s[0]) + j)
    kcol = lambda j, s: (0, 2 * s[3] + s[0])
    pcol = lambda j, s: (0, s[3])
    zero = lambda j, s: (0, 0)
    return pl.pallas_call(
        functools.partial(attend_kernel, heads_per_step),
        grid_spec=pltpu.PrefetchScalarGridSpec(
            num_scalar_prefetch=1,
            grid=(steps,),
            in_specs=[
                pl.BlockSpec((rows, wide), qcol),
                pl.BlockSpec((rows, wide), qcol),
                pl.BlockSpec((1, rows, wide), lambda j, s: (s[3], 0, j)),
                pl.BlockSpec((1, rows, wide), lambda j, s: (s[3], 0, steps + j)),
                pl.BlockSpec((span, HEAD_SIZE), pcol),
                pl.BlockSpec((span, HEAD_SIZE), kcol),
                pl.BlockSpec((span, HEAD_SIZE), pcol),
                pl.BlockSpec((span, HEAD_SIZE), kcol),
                pl.BlockSpec((8, rows), zero),
                pl.BlockSpec((8, rows), zero),
            ],
            out_specs=[
                pl.BlockSpec((rows, wide), lambda j, s: (0, j)),
                pl.BlockSpec((rows, wide), lambda j, s: (0, j)),
                pl.BlockSpec((span, 2 * HEAD_SIZE), zero),
                pl.BlockSpec((span, 2 * HEAD_SIZE), zero),
            ],
            scratch_shapes=[
                pltpu.VMEM((2 * span, 2 * rows), jnp.float32),
                pltpu.VMEM((HEAD_SIZE, 2 * span), jnp.bfloat16),
                pltpu.VMEM((heads_per_step, 2 * span, 2 * rows), jnp.float32),
                pltpu.VMEM((heads_per_step, 2 * span, 2 * rows), jnp.float32),
                pltpu.VMEM((heads_per_step, 2 * span, 2 * rows), jnp.bfloat16),
                pltpu.VMEM((2 * span, HEAD_SIZE), jnp.float32),
                pltpu.VMEM((2 * span, HEAD_SIZE), jnp.float32),
            ],
        ),
        out_shape=[
            jax.ShapeDtypeStruct((rows, SHARE * HEAD_SIZE), jnp.bfloat16),
            jax.ShapeDtypeStruct((rows, SHARE * HEAD_SIZE), jnp.bfloat16),
            jax.ShapeDtypeStruct((span, 2 * HEAD_SIZE), jnp.bfloat16),
            jax.ShapeDtypeStruct((span, 2 * HEAD_SIZE), own_dtype),
        ],
        cost_estimate=pl.CostEstimate(flops=2_400_000_000, bytes_accessed=4_000_000, transcendentals=1_500_000),
        name=name,
    )(jnp.concatenate([scal[:3], which.reshape(1)]), queries, grads, payload, payload, keys_prev, keys, values_prev, values, meta, meta_core)


def place_kernel(s_ref, rows_a, rows_b, meta_a, meta_b, *rest):
    out_ref = rest[-1]
    tokens = rows_a.shape[0]
    local = out_ref.shape[1]

    def emit(rows_ref, meta_ref):
        first = s_ref[2] * (local * CAP)
        slot = (first + lax.broadcasted_iota(jnp.int32, (local * CAP, tokens), 0)).astype(jnp.float32)
        hit0 = slot == meta_ref[0:1]
        hit1 = slot == meta_ref[1:2]
        gate = jnp.sum(
            jnp.where(hit0, meta_ref[2:3], 0.0) + jnp.where(hit1, meta_ref[3:4], 0.0),
            axis=1,
            keepdims=True,
        )
        onehot = (hit0 | hit1).astype(jnp.float32).astype(jnp.bfloat16)
        picked = jnp.dot(onehot, rows_ref[...], preferred_element_type=jnp.float32)
        scaled = (picked * gate).astype(out_ref.dtype)
        for k in range(local):
            out_ref[0, k, 0] = scaled[k * CAP : (k + 1) * CAP]

    step = pl.program_id(0)

    @pl.when(step == 0)
    def _():
        emit(rows_a, meta_a)

    @pl.when(step == 1)
    def _():
        emit(rows_b, meta_b)


def place(scal, rows_a, rows_b, meta_a, meta_b, group, into, name):
    tokens, width = rows_a.shape
    local = EXPERTS // group
    zero = lambda i, s: (0, 0)
    ins = [
        pl.BlockSpec((tokens, width), zero),
        pl.BlockSpec((tokens, width), zero),
        pl.BlockSpec((8, tokens), zero),
        pl.BlockSpec((8, tokens), zero),
    ]
    args = [rows_a, rows_b, meta_a, meta_b]
    alias = {}
    if into is not None:
        ins.append(pl.BlockSpec(memory_space=pl.ANY))
        args.append(into)
        alias = {5: 0}
    return pl.pallas_call(
        place_kernel,
        grid_spec=pltpu.PrefetchScalarGridSpec(
            num_scalar_prefetch=1,
            grid=(2,),
            in_specs=ins,
            out_specs=pl.BlockSpec((1, local, 1, CAP, width), lambda i, s: (0, 0, s[i], 0, 0)),
        ),
        out_shape=jax.ShapeDtypeStruct((1, local, group, CAP, width), rows_a.dtype),
        input_output_aliases=alias,
        cost_estimate=pl.CostEstimate(flops=500_000_000, bytes_accessed=5_200_000, transcendentals=0),
        name=name,
    )(scal, *args)


def finish_kernel(s_ref, own_ref, cross_ref, same_ref, other_ref, near, far, near_part, far_part, k_ref, v_ref, dq_ref):
    total = (
        own_ref[...]
        + cross_ref[...].astype(jnp.float32)
        + same_ref[...].astype(jnp.float32)
        + other_ref[...].astype(jnp.float32)
    ).astype(k_ref.dtype)
    k_ref[...] = total[:, :HEAD_SIZE]
    v_ref[...] = total[:, HEAD_SIZE:]
    wide = SHARE * HEAD_SIZE

    for core in range(2):
        for side in range(2):

            @pl.when((s_ref[0] == core) & (s_ref[1] == side))
            def _():
                for position, mine, part in ((side, near, near_part), (1 - side, far, far_part)):
                    at = 2 * position + core
                    dq_ref[:, at * wide : (at + 1) * wide] = mine[...]
                    at = 2 * position + 1 - core
                    dq_ref[:, at * wide : (at + 1) * wide] = part[...]


def finish(scal, own, cross, same, other, mine0, mine1, part0, part1):
    span = own.shape[0]
    rows, wide = mine0.shape
    zero = lambda i, s: (0, 0)
    args = [own, cross, same, other, mine0, mine1, part0, part1]
    return pl.pallas_call(
        finish_kernel,
        grid_spec=pltpu.PrefetchScalarGridSpec(
            num_scalar_prefetch=1,
            grid=(1,),
            in_specs=[pl.BlockSpec(a.shape, zero) for a in args],
            out_specs=[
                pl.BlockSpec((span, HEAD_SIZE), zero),
                pl.BlockSpec((span, HEAD_SIZE), zero),
                pl.BlockSpec((rows, 4 * wide), zero),
            ],
        ),
        out_shape=[
            jax.ShapeDtypeStruct((span, HEAD_SIZE), jnp.bfloat16),
            jax.ShapeDtypeStruct((span, HEAD_SIZE), jnp.bfloat16),
            jax.ShapeDtypeStruct((rows, 4 * wide), jnp.bfloat16),
        ],
        name="finish",
    )(scal, *args)


def local(
    query_rows,
    key_rows,
    value_matrix,
    out_grads,
    doc_start,
    moe_grads,
    expert_out,
    gate_logits,
    routes,
):
    rows = query_rows.shape[0]
    group = lax.axis_size("exp")
    ctx_pos = lax.axis_index("ctx").astype(jnp.int32)
    exp_pos = lax.axis_index("exp").astype(jnp.int32)
    core = exp_pos % 2
    side = exp_pos // 2
    scal = jnp.stack([core, side, ctx_pos])

    kpay, vpay = pack_kv(scal, key_rows, value_matrix)
    keys_prev = send(kpay, to_next_same)
    values_prev = send(vpay, to_next_other)
    payload, meta = pack_qg(
        scal, query_rows, out_grads, gate_logits.T, routes.T, doc_start.reshape(1, rows)
    )
    payload = send(payload, to_core)
    meta_core = send(meta, to_core)
    meta_cross = send(meta, to_cross)
    meta_diag = send(meta_cross, to_core)
    rows_cross = send(moe_grads, to_cross)
    rows_core = send(moe_grads, to_core)
    rows_diag = send(rows_cross, to_core)

    gate = jax.nn.sigmoid(gate_logits - gate_logits[:, ::-1])
    gate_grad = jnp.einsum("td,tad->ta", moe_grads, expert_out, preferred_element_type=jnp.float32)
    logit_grads = gate * (gate_grad - jnp.sum(gate * gate_grad, axis=-1, keepdims=True))

    near = place(
        jnp.stack([exp_pos, exp_pos ^ 1, exp_pos]), moe_grads, rows_core, meta, meta_core, group, None, "place_near"
    )
    both = functools.partial(
        attend, scal, query_rows, out_grads, payload, keys_prev, key_rows, values_prev, value_matrix, meta, meta_core
    )
    dqo_far, dqp_far, prev_far, own_far = both(1 - side, jnp.bfloat16, "attend_far")
    cross = send(own_far, to_cross)
    back_other = send(prev_far, to_prev_other)
    part_far = send(dqp_far, to_core)
    dqo_near, dqp_near, prev_near, own_near = both(side, jnp.float32, "attend_near")
    back_same = send(prev_near, to_prev_same)
    part_near = send(dqp_near, to_core)

    expert_grads = place(
        jnp.stack([exp_pos ^ 2, exp_pos ^ 3, exp_pos]), rows_cross, rows_diag, meta_cross, meta_diag, group, near, "place_far"
    )
    key_grads, value_grads, query_grads = finish(
        jnp.stack([core, side]), own_near, cross, back_same, back_other, dqo_near, dqo_far, part_near, part_far
    )
    return (query_grads, key_grads, value_grads, expert_grads, logit_grads)


def solution(mesh):
    in_specs = (
        P(("ctx", "exp"), None),
        P("ctx", None),
        P("ctx", None),
        P(("ctx", "exp"), None),
        P(("ctx", "exp")),
        P(("ctx", "exp"), None),
        P(("ctx", "exp"), None, None),
        P(("ctx", "exp"), None),
        P(("ctx", "exp"), None),
    )
    out_specs = (
        P(("ctx", "exp"), None),
        P("ctx", "exp"),
        P("ctx", "exp"),
        P("ctx", "exp", None, None, None),
        P(("ctx", "exp"), None),
    )
    return jax.shard_map(local, mesh=mesh, in_specs=in_specs, out_specs=out_specs, check_vma=False)
```

time: 218 us -> 117 us (0.54)
  the two profiles are of different devices: /device:TPU:103 before, /device:TPU:1 now
where the time goes in v1:
time: 117 us
  waiting for transfers between devices  44.5 us (38%)
  Pallas kernels  38.8 us (33%)
  starting transfers between devices  19.2 us (16%)
  matrix products  8.62 us (7%)
  other arithmetic  4.36 us (4%)
    ppermute x14, waiting for transfers between devices, send(): return lax.ppermute(x, AXES, routes_of(fn))  44.5 us
    pallas_call x2, Pallas kernels, attend(): pl.pallas_call(functools.partial(attend_kernel, heads_per_step), grid_spe...  21.5 us
    ppermute x14, starting transfers between devices, send(): return lax.ppermute(x, AXES, routes_of(fn))  19.2 us
    pallas_call x2, Pallas kernels, place(): pl.pallas_call(place_kernel, grid_spec=pltpu.PrefetchScalarGridSpec(num_s...  8.79 us
    dot_general x1, matrix products, local(): jnp.einsum('td,tad->ta', moe_grads, expert_out, preferred_element_type=jn...  8.62 us
    pallas_call x1, Pallas kernels, finish(): pl.pallas_call(finish_kernel, grid_spec=pltpu.PrefetchScalarGridSpec(num_...  3.31 us
    pallas_call x1, Pallas kernels, pack_qg(): pl.pallas_call(pack_qg_kernel, grid_spec=pltpu.PrefetchScalarGridSpec(num...  2.76 us
    pallas_call x1, Pallas kernels, pack_kv(): pl.pallas_call(pack_kv_kernel, grid_spec=pltpu.PrefetchScalarGridSpec(num...  2.52 us
  transfers between devices with their start and end apart: 14, of which 3 were waited for; matrix products, arithmetic and copies ran while one was open for 11% of the time, Pallas kernels for 29%

profile of v1, /device:TPU:1, one launch (start us, length us, event | category | flops | bytes accessed | tf_op | source)
XLA Modules:
  0.0 116.9 jit_solution(11360459932928759543)
XLA Ops:
  0.6 3.3 %collective-permute-start.13 = (bf16[128,6144]{1,0:T(8,128)(2,1)}, bf16[128,6144]{1,0:T(8,128)(2,1)}, u32[]{:S(2)}, u32[]{:S(2)}) collective-permute-start(bf16[128,6144]{1,0:T(8,128)(2,1)} %rows_a.1), channel_id=1, source_target_pairs={{0,1},{1,0},{2,3},{3,2},{4,5},{5,4},{6,7},{7,6},{8,9},{9,8},{10,11... | collective-permute-start | bytes 4718600 | tf_op jit(solution)/shard_map/ppermute | solution.py:34
  3.9 1.2 %collective-permute-start.9 = (bf16[128,6144]{1,0:T(8,128)(2,1)}, bf16[128,6144]{1,0:T(8,128)(2,1)}, u32[]{:S(2)}, u32[]{:S(2)}) collective-permute-start(bf16[128,6144]{1,0:T(8,128)(2,1)} %rows_a.1), channel_id=1, source_target_pairs={{0,2},{1,3},{2,0},{3,1},{4,6},{5,7},{6,4},{7,5},{8,10},{9,11},{10,... | collective-permute-start | bytes 4718600 | tf_op jit(solution)/shard_map/ppermute | solution.py:34
  5.1 0.6 pad_add_fusion.3.s_ref
  5.7 2.8 %pack_qg.1 = (bf16[2,128,1536]{2,1,0:T(8,128)(2,1)}, f32[8,128]{1,0:T(8,128)}) custom-call(s32[3]{0:T(128)} %pad_add_fusion.3.s_ref, bf16[128,3072]{1,0:T(8,128)(2,1)} %q_ref.5, bf16[128,3072]{1,0:T(8,128)(2,1)} %g_ref.5, f32[2,128]{1,0:T(2,128)} %bitcast.21, s32[2,128]{1,0:T(2,128)} %bitcast.22, s32[1,128]{1,0:T(1,128)} %bitcast.23), custom_call_target="tpu_custom_call" | custom-call | tf_op jit(solution)/shard_map/pack_qg/pallas_call | solution.py:120
  8.5 0.4 collective-permute-start.3
  8.9 0.1 collective-permute-start
  9.0 2.5 %pack_kv.1 = (bf16[512,256]{1,0:T(8,128)(2,1)}, bf16[512,256]{1,0:T(8,128)(2,1)}) custom-call(s32[3]{0:T(128)} %pad_add_fusion.3.s_ref, bf16[512,512]{1,0:T(8,128)(2,1)} %ko_ref.3, bf16[512,512]{1,0:T(8,128)(2,1)} %vo_ref.3), custom_call_target="tpu_custom_call" | custom-call | tf_op jit(solution)/shard_map/pack_kv/pallas_call | solution.py:72
  11.5 0.4 collective-permute-start.1
  11.9 8.6 %fusion = f32[128,1,2]{2,1,0:T(1,128)S(1)} fusion(bf16[128,2,6144]{2,1,0:T(2,128)(2,1)S(1)} %copy-done, bf16[128,6144,1]{1,0,2:T(8,128)(2,1)} %bitcast.20), kind=kOutput, calls=%fused_computation | convolution fusion | flops 3145728 | bytes 4719616 | tf_op jit(solution)/shard_map/td,tad->ta/dot_general | solution.py:453
  20.5 21.1 %collective-permute-done.9.rows_a = bf16[128,6144]{1,0:T(8,128)(2,1)} collective-permute-done((bf16[128,6144]{1,0:T(8,128)(2,1)}, bf16[128,6144]{1,0:T(8,128)(2,1)}, u32[]{:S(2)}, u32[]{:S(2)}) %collective-permute-start.9) | collective-permute-done | bytes 1572896 | tf_op jit(solution)/shard_map/ppermute | solution.py:34
  41.6 1.5 %collective-permute-start.10 = (bf16[128,6144]{1,0:T(8,128)(2,1)}, bf16[128,6144]{1,0:T(8,128)(2,1)}, u32[]{:S(2)}, u32[]{:S(2)}) collective-permute-start(bf16[128,6144]{1,0:T(8,128)(2,1)} %collective-permute-done.9.rows_a), channel_id=1, source_target_pairs={{0,1},{1,0},{2,3},{3,2},{4,5},{5,4},{6,7},{7,6},{8,9},{9,8},{10,11... | collective-permute-start | bytes 4718600 | tf_op jit(solution)/shard_map/ppermute | solution.py:34
  43.1 0.7 pad_add_fusion.4
  43.8 6.1 %collective-permute-start.2 = (bf16[512,256]{1,0:T(8,128)(2,1)}, bf16[512,256]{1,0:T(8,128)(2,1)}, u32[]{:S(2)}, u32[]{:S(2)}) collective-permute-start(bf16[512,256]{1,0:T(8,128)(2,1)} %get-tuple-element.22), channel_id=1, source_target_pairs={{0,6},{1,7},{2,4},{3,5},{4,10},{5,11},{6,8},{7,9},{8,14},{9,15},{1... | collective-permute-start | bytes 786440 | tf_op jit(solution)/shard_map/ppermute | solution.py:34
  49.9 0.6 pad_add_fusion.1.s_ref
  50.6 0.4 collective-permute-start.11
  51.1 13.3 %collective-permute-done.2.vp_ref = bf16[512,256]{1,0:T(8,128)(2,1)} collective-permute-done((bf16[512,256]{1,0:T(8,128)(2,1)}, bf16[512,256]{1,0:T(8,128)(2,1)}, u32[]{:S(2)}, u32[]{:S(2)}) %collective-permute-start.2) | collective-permute-done | bytes 262176 | tf_op jit(solution)/shard_map/ppermute | solution.py:34
  64.4 10.7 %attend_far.1 = (bf16[128,768]{1,0:T(8,128)(2,1)}, bf16[128,768]{1,0:T(8,128)(2,1)}, bf16[512,256]{1,0:T(8,128)(2,1)}, bf16[512,256]{1,0:T(8,128)(2,1)}) custom-call(s32[4]{0:T(128)} %get-tuple-element.37.s_ref, bf16[128,3072]{1,0:T(8,128)(2,1)} %q_ref.5, bf16[128,3072]{1,0:T(8,128)(2,1)} %g_ref.5, bf16[2,128,1536]{2,1,0:T(8,128)(2,1)} %collective-permute-done.qp_ref.gp_ref, ...), custom_call_target="tpu_custom_call" | custom-call | flops 2400000000 | bytes 4000000 | tf_op jit(solution)/shard_map/attend_far/pallas_call | solution.py:263
  75.1 0.8 collective-permute-start.8
  75.9 10.8 %attend_near.1 = (bf16[128,768]{1,0:T(8,128)(2,1)}, bf16[128,768]{1,0:T(8,128)(2,1)}, bf16[512,256]{1,0:T(8,128)(2,1)}, f32[512,256]{1,0:T(8,128)}) custom-call(s32[4]{0:T(128)} %pad_add_fusion.1.s_ref, bf16[128,3072]{1,0:T(8,128)(2,1)} %q_ref.5, bf16[128,3072]{1,0:T(8,128)(2,1)} %g_ref.5, bf16[2,128,1536]{2,1,0:T(8,128)(2,1)} %collective-permute-done.qp_ref.gp_ref, ...), custom_call_target="tpu_custom_call" | custom-call | flops 2400000000 | bytes 4000000 | tf_op jit(solution)/shard_map/attend_near/pallas_call | solution.py:263
  86.8 0.6 pad_add_fusion.s_ref
  87.4 0.7 add_add_fusion.1.s_ref
  88.1 0.4 collective-permute-start.4
  88.5 2.5 %collective-permute-start.6 = (bf16[512,256]{1,0:T(8,128)(2,1)}, bf16[512,256]{1,0:T(8,128)(2,1)}, u32[]{:S(2)}, u32[]{:S(2)}) collective-permute-start(bf16[512,256]{1,0:T(8,128)(2,1)} %get-tuple-element.27), channel_id=1, source_target_pairs={{0,254},{1,255},{2,252},{3,253},{4,2},{5,3},{6,0},{7,1},{8,6},{9,7... | collective-permute-start | bytes 786440 | tf_op jit(solution)/shard_map/ppermute | solution.py:34
  91.0 0.6 collective-permute-start.5
  91.6 0.6 add_add_fusion.s_ref
  92.2 0.6 fusion.3
  92.7 10.1 %collective-permute-done.4.cross_ref = bf16[512,256]{1,0:T(8,128)(2,1)S(1)} collective-permute-done((bf16[512,256]{1,0:T(8,128)(2,1)}, bf16[512,256]{1,0:T(8,128)(2,1)S(1)}, u32[]{:S(2)}, u32[]{:S(2)}) %collective-permute-start.4) | collective-permute-done | bytes 262176 | tf_op jit(solution)/shard_map/ppermute | solution.py:34
  102.9 1.3 %collective-permute-start.12 = (f32[8,128]{1,0:T(8,128)S(1)}, f32[8,128]{1,0:T(8,128)S(1)}, u32[]{:S(2)}, u32[]{:S(2)}) collective-permute-start(f32[8,128]{1,0:T(8,128)S(1)} %collective-permute-done.11.meta_a), channel_id=1, source_target_pairs={{0,1},{1,0},{2,3},{3,2},{4,5},{5,4},{6,7},{7,6},{8,9},{9,8},{10,11... | collective-permute-start | bytes 12296 | tf_op jit(solution)/shard_map/ppermute | solution.py:34
  104.2 3.3 %finish.1 = (bf16[512,128]{1,0:T(8,128)(2,1)}, bf16[512,128]{1,0:T(8,128)(2,1)}, bf16[128,3072]{1,0:T(8,128)(2,1)}) custom-call(s32[2]{0:T(128)} %pad_add_fusion.s_ref, f32[512,256]{1,0:T(8,128)} %get-tuple-element.24.own_ref, bf16[512,256]{1,0:T(8,128)(2,1)} %copy-done.1, bf16[512,256]{1,0:T(8,128)(2,1)} %collective-permute-done.5.same_ref, ...), custom_call_target="tpu_custom_call" | custom-call | tf_op jit(solution)/shard_map/finish/pallas_call | solution.py:398
  107.5 4.4 %place_near.1.rest_0_ = bf16[1,2,4,40,6144]{4,3,2,1,0:T(8,128)(2,1)} custom-call(s32[3]{0:T(128)} %add_add_fusion.1.s_ref, bf16[128,6144]{1,0:T(8,128)(2,1)} %rows_a.1, bf16[128,6144]{1,0:T(8,128)(2,1)} %collective-permute-done.13.rows_b, f32[8,128]{1,0:T(8,128)} %get-tuple-element.23.meta_ref.meta_a, f32[8,128]{1,0:T(8,128)} %copy-done.4), custom_call_target="tpu_custom_call" | custom-call | flops 500000000 | bytes 5200000 | tf_op jit(solution)/shard_map/place_near/pallas_call | solution.py:355
  112.0 0.6 copy-done.6
  112.5 4.4 %place_far.1 = bf16[1,2,4,40,6144]{4,3,2,1,0:T(8,128)(2,1)} custom-call(s32[3]{0:T(128)} %add_add_fusion.s_ref, bf16[128,6144]{1,0:T(8,128)(2,1)} %collective-permute-done.9.rows_a, bf16[128,6144]{1,0:T(8,128)(2,1)} %collective-permute-done.10.rows_b, f32[8,128]{1,0:T(8,128)} %copy-done.5, f32[8,128]{1,0:T(8,128)} %copy-done.6, ...), custom_call_target="tpu_custom_call", output_to_operand_aliasing={{}: (5, {})} | custom-call | flops 500000000 | bytes 5200000 | tf_op jit(solution)/shard_map/place_far/pallas_call | solution.py:355
  (30 shorter events, 0.3 us)
Async XLA Ops:
  0.6 11.3 %copy-start = (bf16[128,2,6144]{2,1,0:T(2,128)(2,1)S(1)}, bf16[128,2,6144]{2,1,0:T(2,128)(2,1)}, u32[]{:S(2)}) copy-start(bf16[128,2,6144]{2,1,0:T(2,128)(2,1)} %param.15) | copy-start | bytes 9437188
  0.6 106.9 %collective-permute-start.13 = (bf16[128,6144]{1,0:T(8,128)(2,1)}, bf16[128,6144]{1,0:T(8,128)(2,1)}, u32[]{:S(2)}, u32[]{:S(2)}) collective-permute-start(bf16[128,6144]{1,0:T(8,128)(2,1)} %rows_a.1), channel_id=1, source_target_pairs={{0,1},{1,0},{2,3},{3,2},{4,5},{5,4},{6,7},{7,6},{8,9},{9,8},{10,11... | collective-permute-start | bytes 4718600 | tf_op jit(solution)/shard_map/ppermute | solution.py:34
  3.9 37.7 %collective-permute-start.9 = (bf16[128,6144]{1,0:T(8,128)(2,1)}, bf16[128,6144]{1,0:T(8,128)(2,1)}, u32[]{:S(2)}, u32[]{:S(2)}) collective-permute-start(bf16[128,6144]{1,0:T(8,128)(2,1)} %rows_a.1), channel_id=1, source_target_pairs={{0,2},{1,3},{2,0},{3,1},{4,6},{5,7},{6,4},{7,5},{8,10},{9,11},{10,... | collective-permute-start | bytes 4718600 | tf_op jit(solution)/shard_map/ppermute | solution.py:34
  8.5 35.3 %collective-permute-start.3 = (f32[8,128]{1,0:T(8,128)}, f32[8,128]{1,0:T(8,128)S(1)}, u32[]{:S(2)}, u32[]{:S(2)}) collective-permute-start(f32[8,128]{1,0:T(8,128)} %get-tuple-element.23.meta_ref.meta_a), channel_id=1, source_target_pairs={{0,1},{1,0},{2,3},{3,2},{4,5},{5,4},{6,7},{7,6},{8,9},{9,8},{10,11... | collective-permute-start | bytes 12296 | tf_op jit(solution)/shard_map/ppermute | solution.py:34
  8.9 55.5 %collective-permute-start = (bf16[2,128,1536]{2,1,0:T(8,128)(2,1)}, bf16[2,128,1536]{2,1,0:T(8,128)(2,1)}, u32[]{:S(2)}, u32[]{:S(2)}) collective-permute-start(bf16[2,128,1536]{2,1,0:T(8,128)(2,1)} %get-tuple-element.20), channel_id=1, source_target_pairs={{0,1},{1,0},{2,3},{3,2},{4,5},{5,4},{6,7},{7,6},{8,9},{9,8},{10,11... | collective-permute-start | bytes 2359304 | tf_op jit(solution)/shard_map/ppermute | solution.py:34
  11.5 39.1 %collective-permute-start.1 = (bf16[512,256]{1,0:T(8,128)(2,1)}, bf16[512,256]{1,0:T(8,128)(2,1)S(1)}, u32[]{:S(2)}, u32[]{:S(2)}) collective-permute-start(bf16[512,256]{1,0:T(8,128)(2,1)} %get-tuple-element.21), channel_id=1, source_target_pairs={{0,4},{1,5},{2,6},{3,7},{4,8},{5,9},{6,10},{7,11},{8,12},{9,13},{1... | collective-permute-start | bytes 786440 | tf_op jit(solution)/shard_map/ppermute | solution.py:34
  11.9 38.6 %copy-start.2 = (f32[128,2]{0,1:T(2,128)S(1)}, f32[128,2]{0,1:T(2,128)}, u32[]{:S(2)}) copy-start(f32[128,2]{0,1:T(2,128)} %param.16) | copy-start | bytes 3076
  11.9 38.7 %copy-start.3 = (f32[8,128]{1,0:T(8,128)S(1)}, f32[8,128]{1,0:T(8,128)}, u32[]{:S(2)}) copy-start(f32[8,128]{1,0:T(8,128)} %get-tuple-element.23.meta_ref.meta_a) | copy-start | bytes 12292
  41.6 70.3 %collective-permute-start.10 = (bf16[128,6144]{1,0:T(8,128)(2,1)}, bf16[128,6144]{1,0:T(8,128)(2,1)}, u32[]{:S(2)}, u32[]{:S(2)}) collective-permute-start(bf16[128,6144]{1,0:T(8,128)(2,1)} %collective-permute-done.9.rows_a), channel_id=1, source_target_pairs={{0,1},{1,0},{2,3},{3,2},{4,5},{5,4},{6,7},{7,6},{8,9},{9,8},{10,11... | collective-permute-start | bytes 4718600 | tf_op jit(solution)/shard_map/ppermute | solution.py:34
  43.8 20.6 %copy-start.4 = (f32[8,128]{1,0:T(8,128)}, f32[8,128]{1,0:T(8,128)S(1)}, u32[]{:S(2)}) copy-start(f32[8,128]{1,0:T(8,128)S(1)} %collective-permute-done.3.metap_ref.meta_b) | copy-start | bytes 12292
  43.8 20.6 %collective-permute-start.2 = (bf16[512,256]{1,0:T(8,128)(2,1)}, bf16[512,256]{1,0:T(8,128)(2,1)}, u32[]{:S(2)}, u32[]{:S(2)}) collective-permute-start(bf16[512,256]{1,0:T(8,128)(2,1)} %get-tuple-element.22), channel_id=1, source_target_pairs={{0,6},{1,7},{2,4},{3,5},{4,10},{5,11},{6,8},{7,9},{8,14},{9,15},{1... | collective-permute-start | bytes 786440 | tf_op jit(solution)/shard_map/ppermute | solution.py:34
  50.6 13.7 %copy-start.7 = (bf16[512,256]{1,0:T(8,128)(2,1)}, bf16[512,256]{1,0:T(8,128)(2,1)S(1)}, u32[]{:S(2)}) copy-start(bf16[512,256]{1,0:T(8,128)(2,1)S(1)} %collective-permute-done.1.kp_ref) | copy-start | bytes 786436
  50.6 37.5 %collective-permute-start.11 = (f32[8,128]{1,0:T(8,128)S(1)}, f32[8,128]{1,0:T(8,128)S(1)}, u32[]{:S(2)}, u32[]{:S(2)}) collective-permute-start(f32[8,128]{1,0:T(8,128)S(1)} %copy-done.3), channel_id=1, source_target_pairs={{0,2},{1,3},{2,0},{3,1},{4,6},{5,7},{6,4},{7,5},{8,10},{9,11},{10,... | collective-permute-start | bytes 12296 | tf_op jit(solution)/shard_map/ppermute | solution.py:34
  75.1 13.4 %collective-permute-start.8 = (bf16[128,768]{1,0:T(8,128)(2,1)}, bf16[128,768]{1,0:T(8,128)(2,1)}, u32[]{:S(2)}, u32[]{:S(2)}) collective-permute-start(bf16[128,768]{1,0:T(8,128)(2,1)} %get-tuple-element.31), channel_id=1, source_target_pairs={{0,1},{1,0},{2,3},{3,2},{4,5},{5,4},{6,7},{7,6},{8,9},{9,8},{10,11... | collective-permute-start | bytes 589832 | tf_op jit(solution)/shard_map/ppermute | solution.py:34
  86.7 4.3 %collective-permute-start.7 = (bf16[128,768]{1,0:T(8,128)(2,1)}, bf16[128,768]{1,0:T(8,128)(2,1)}, u32[]{:S(2)}, u32[]{:S(2)}) collective-permute-start(bf16[128,768]{1,0:T(8,128)(2,1)} %get-tuple-element.30), channel_id=1, source_target_pairs={{0,1},{1,0},{2,3},{3,2},{4,5},{5,4},{6,7},{7,6},{8,9},{9,8},{10,11... | collective-permute-start | bytes 589832 | tf_op jit(solution)/shard_map/ppermute | solution.py:34
  88.1 23.8 %copy-start.5 = (f32[8,128]{1,0:T(8,128)}, f32[8,128]{1,0:T(8,128)S(1)}, u32[]{:S(2)}) copy-start(f32[8,128]{1,0:T(8,128)S(1)} %collective-permute-done.11.meta_a) | copy-start | bytes 12292
  88.1 14.8 %collective-permute-start.4 = (bf16[512,256]{1,0:T(8,128)(2,1)}, bf16[512,256]{1,0:T(8,128)(2,1)S(1)}, u32[]{:S(2)}, u32[]{:S(2)}) collective-permute-start(bf16[512,256]{1,0:T(8,128)(2,1)} %get-tuple-element.25), channel_id=1, source_target_pairs={{0,2},{1,3},{2,0},{3,1},{4,6},{5,7},{6,4},{7,5},{8,10},{9,11},{10,... | collective-permute-start | bytes 786440 | tf_op jit(solution)/shard_map/ppermute | solution.py:34
  88.5 15.7 %collective-permute-start.6 = (bf16[512,256]{1,0:T(8,128)(2,1)}, bf16[512,256]{1,0:T(8,128)(2,1)}, u32[]{:S(2)}, u32[]{:S(2)}) collective-permute-start(bf16[512,256]{1,0:T(8,128)(2,1)} %get-tuple-element.27), channel_id=1, source_target_pairs={{0,254},{1,255},{2,252},{3,253},{4,2},{5,3},{6,0},{7,1},{8,6},{9,7... | collective-permute-start | bytes 786440 | tf_op jit(solution)/shard_map/ppermute | solution.py:34
  91.0 13.2 %collective-permute-start.5 = (bf16[512,256]{1,0:T(8,128)(2,1)}, bf16[512,256]{1,0:T(8,128)(2,1)}, u32[]{:S(2)}, u32[]{:S(2)}) collective-permute-start(bf16[512,256]{1,0:T(8,128)(2,1)} %get-tuple-element.26), channel_id=1, source_target_pairs={{0,252},{1,253},{2,254},{3,255},{4,0},{5,1},{6,2},{7,3},{8,4},{9,5... | collective-permute-start | bytes 786440 | tf_op jit(solution)/shard_map/ppermute | solution.py:34
  102.9 1.3 %copy-start.1 = (bf16[512,256]{1,0:T(8,128)(2,1)}, bf16[512,256]{1,0:T(8,128)(2,1)S(1)}, u32[]{:S(2)}) copy-start(bf16[512,256]{1,0:T(8,128)(2,1)S(1)} %collective-permute-done.4.cross_ref) | copy-start | bytes 786436
  102.9 9.1 %collective-permute-start.12 = (f32[8,128]{1,0:T(8,128)S(1)}, f32[8,128]{1,0:T(8,128)S(1)}, u32[]{:S(2)}, u32[]{:S(2)}) collective-permute-start(f32[8,128]{1,0:T(8,128)S(1)} %collective-permute-done.11.meta_a), channel_id=1, source_target_pairs={{0,1},{1,0},{2,3},{3,2},{4,5},{5,4},{6,7},{7,6},{8,9},{9,8},{10,11... | collective-permute-start | bytes 12296 | tf_op jit(solution)/shard_map/ppermute | solution.py:34
  111.9 0.6 copy-start.6
